TPU v7x, 32 devices: a whole 2x2x4 slice. The times are simulated.
32 devices in a mesh: blen: 4 (over z), tm: 8 (over y, x, core).
Axes of the slice: x: 2, y: 2, z: 4, core: 2. Of those that a mesh axis runs over, the one named last changes fastest.
Arguments:
- model_grid: bfloat16 [256, 2, 512, 512], P(('blen', 'tm')), may hold values from -6 to 6
- vis_values: float32 [2, 16384], P(None, ('blen', 'tm')), may hold values from -6 to 6
- weights: float32 [16384], P(('blen', 'tm')), may hold values from 0.3 to 3
- flags: int32 [16384], P(('blen', 'tm')), may hold values 0 or 1
- uv_frac: float32 [2, 16384], P(None, ('blen', 'tm')), may hold values from 0 to 1
- cell_offset: int32 [2, 16384], P(None, ('blen', 'tm')), may hold values from 3 to 507
- tile_index: int32 [16384, 1], P(('blen', 'tm')), may hold values from 0 to 255; in each aligned block of 512 rows (0 to 511, 512 to 1023, ...) at most 4 rows name the same one
Outputs:
- gradient: float32 [8192, 8192], P(('blen', 'tm'))
- weighted_residual: float32 [2, 16384], P(None, ('blen', 'tm'))
Inputs may be any that keep to these rules, and one draw needn't show every extreme that they name: `tile_index`: in the rows of one device no tile is named by more than 4 rows, and some device has a tile named by exactly 4 rows.
All inputs are finite; a program needn't handle non-finite values. No bound on the sum of `flags` on one device may be relied on, other than what follows from the above.
Results may differ from a plain program's by a relative error of at most 0.0095.
Values sent between devices are 32-bit elements; how exact they have to be, the bound alone decides.
No kernel may reach another device: no remote copies, remote signals or barrier semaphores. Data moves between devices by JAX's collectives and lax.ppermute only.
A program may use at most 192 MiB of HBM per device.

v0:
```python
import math
import jax
import jax.numpy as jnp
from jax import lax
from jax.sharding import PartitionSpec as P

NPIX = 8192
KSUP = 8
NT = 16
MOST = 4
kernel_scale = 0.5
highest = lax.Precision.HIGHEST


def taps_full(offsets, fractions, tile_side):
    cell_ids = lax.broadcasted_iota(jnp.int32, offsets.shape + (tile_side,), offsets.ndim)
    shifted = cell_ids - offsets[..., None]
    distance = shifted.astype(jnp.float32) - fractions[..., None]
    inside = (shifted >= 1 - KSUP // 2) & (shifted <= KSUP // 2)
    values = jnp.exp(-kernel_scale * distance * distance)
    return jnp.where(inside, values, 0.0).astype(jnp.bfloat16)


def phase_table(row_count, col_count, period):
    row_ids = lax.broadcasted_iota(jnp.int32, (row_count, col_count), 0)
    col_ids = lax.broadcasted_iota(jnp.int32, (row_count, col_count), 1)
    angles = 2.0 * math.pi / period * (row_ids * col_ids % period).astype(jnp.float32)
    return (jnp.cos(angles), jnp.sin(angles))


def complex_block(cos_part, sin_part):
    return jnp.stack([jnp.stack([cos_part, -sin_part]), jnp.stack([sin_part, cos_part])])


def on_device(model_grid, vis_values, weights, flags, uv_frac, cell_offset, tile_index):
    blen_size = lax.axis_size("blen")
    tm_size = lax.axis_size("tm")
    devices = blen_size * tm_size
    per_dev = model_grid.shape[0]
    tile_side = model_grid.shape[2]
    vis_count = weights.shape[0]
    ntiles = per_dev * devices
    total_slots = ntiles * MOST
    tile_ids = tile_index[:, 0]
    matches = tile_ids[:, None] == lax.broadcasted_iota(jnp.int32, (vis_count, ntiles), 1)
    counts = jnp.sum(matches.astype(jnp.int32), axis=0)
    starts = jnp.cumsum(counts) - counts
    sorting = jnp.argsort(tile_ids, stable=True)
    position = (
        jnp.zeros((vis_count,), jnp.int32).at[sorting].set(jnp.arange(vis_count, dtype=jnp.int32))
    )
    first_slot = jnp.sum(jnp.where(matches, starts[None, :], 0), axis=1)
    rank_in_tile = position - first_slot
    owner_dev = tile_ids // per_dev
    local_tile = tile_ids % per_dev
    slot_of = (local_tile * devices + owner_dev) * MOST + rank_in_tile
    weighted = weights * flags.astype(jnp.float32)
    float_fields = jnp.stack([vis_values[0], vis_values[1], weighted, uv_frac[0], uv_frac[1]])
    send_float = jnp.zeros((5, total_slots), jnp.float32).at[:, slot_of].set(float_fields)
    send_int = jnp.zeros((2, total_slots), jnp.int32).at[:, slot_of].set(cell_offset)
    recv_float, recv_int = (
        lax.all_to_all(
            send_float.reshape(5, per_dev, devices, MOST),
            ("blen", "tm"),
            split_axis=2,
            concat_axis=2,
            tiled=True,
        ),
        lax.all_to_all(
            send_int.reshape(2, per_dev, devices, MOST),
            ("blen", "tm"),
            split_axis=2,
            concat_axis=2,
            tiled=True,
        ),
    )
    owner_rows = devices * MOST
    block_rows = 512 if owner_rows % 512 == 0 else owner_rows
    block_count = owner_rows // block_rows
    float_blocks = recv_float.reshape(5, per_dev, block_count, block_rows).transpose(2, 0, 1, 3)
    int_blocks = recv_int.reshape(2, per_dev, block_count, block_rows).transpose(2, 0, 1, 3)

    def grid_step(adjoint, inputs):
        part_float, part_int = inputs
        taps_u = taps_full(part_int[0], part_float[3], tile_side)
        taps_v = taps_full(part_int[1], part_float[4], tile_side)
        partial_sums = jnp.einsum(
            "qrj,qcji->qrci", taps_v, model_grid, preferred_element_type=jnp.float32
        )
        predicted = jnp.sum(partial_sums * taps_u[:, :, None, :], axis=-1)
        observed = jnp.stack([part_float[0], part_float[1]], axis=-1)
        residual = part_float[2][..., None] * (predicted - observed)
        spread = (residual[..., None] * taps_u[:, :, None, :]).astype(jnp.bfloat16)
        adjoint = adjoint + jnp.einsum(
            "qrj,qrci->qcji", taps_v, spread, preferred_element_type=jnp.float32
        )
        return (adjoint, jnp.moveaxis(residual, -1, 0))

    start_adjoint = jnp.zeros((per_dev, 2, tile_side, tile_side), jnp.float32)
    adjoint, residual_blocks = lax.scan(grid_step, start_adjoint, (float_blocks, int_blocks))
    residual_slots = residual_blocks.transpose(1, 2, 0, 3).reshape(2, per_dev, owner_rows)
    returned = lax.all_to_all(
        residual_slots.reshape(2, per_dev, devices, MOST),
        ("blen", "tm"),
        split_axis=2,
        concat_axis=2,
        tiled=True,
    )
    weighted_residual = returned.reshape(2, total_slots)[:, slot_of]
    relaid = lax.all_to_all(adjoint, "tm", split_axis=2, concat_axis=0, tiled=True)
    tile_cols = NT // blen_size
    col_slice = tile_side // tm_size
    pieces = relaid.reshape(NT, tile_cols, 2, col_slice, tile_side)
    cos_small, sin_small = phase_table(NT, NT, NT)
    small_turn = complex_block(cos_small, sin_small)
    cos_twist, sin_twist = phase_table(NT, tile_side, NPIX)
    cos_tile, sin_tile = phase_table(tile_side, tile_side, tile_side)
    tile_turn = complex_block(cos_tile, sin_tile)
    section_one = jnp.einsum("acnt,tvcji->anvji", small_turn, pieces, precision=highest)
    twist_c = cos_twist[:, None, None, :]
    twist_s = sin_twist[:, None, None, :]
    turned = jnp.stack(
        [
            section_one[0] * twist_c - section_one[1] * twist_s,
            section_one[0] * twist_s + section_one[1] * twist_c,
        ]
    )
    columns = jnp.einsum("acmi,cnvji->amnvj", tile_turn, turned, precision=highest)
    rows_dev = NPIX // devices
    spread_cols = rows_dev * tile_cols * col_slice
    packed = columns.reshape(2, 1, devices, spread_cols)
    landed = lax.all_to_all(packed, ("blen", "tm"), split_axis=2, concat_axis=1, tiled=True)
    landed = landed.reshape(2, blen_size, tm_size, rows_dev, tile_cols, col_slice)
    small_split = small_turn.reshape(2, 2, NT, blen_size, tile_cols)
    section_two = jnp.einsum("acnpv,cptrvj->antrj", small_split, landed, precision=highest)
    twist_cv = cos_twist.reshape(NT, tm_size, 1, col_slice)
    twist_sv = sin_twist.reshape(NT, tm_size, 1, col_slice)
    turned_rows = jnp.stack(
        [
            section_two[0] * twist_cv - section_two[1] * twist_sv,
            section_two[0] * twist_sv + section_two[1] * twist_cv,
        ]
    )
    real_turn = jnp.stack([cos_tile, -sin_tile]).reshape(2, tile_side, tm_size, col_slice)
    image_rows = jnp.einsum("cmtj,cntrj->rmn", real_turn, turned_rows, precision=highest)
    gradient = image_rows.reshape(rows_dev, NPIX) / NPIX
    return (gradient, weighted_residual)


def solution(mesh):
    in_specs = (
        P(("blen", "tm"), None, None, None),
        P(None, ("blen", "tm")),
        P(("blen", "tm")),
        P(("blen", "tm")),
        P(None, ("blen", "tm")),
        P(None, ("blen", "tm")),
        P(("blen", "tm"), None),
    )
    out_specs = (P(("blen", "tm"), None), P(None, ("blen", "tm")))
    return jax.shard_map(
        on_device, mesh=mesh, in_specs=in_specs, out_specs=out_specs, check_vma=False
    )
```

profile of v0, /device:TPU:0, one launch (start us, length us, event | category | flops | bytes accessed | tf_op | source)
XLA Modules:
  0.0 1047.1 jit_solution(14593329809357333968)
XLA Ops:
  3.0 4.4 sort.17
  14.8 7.3 all-to-all-start.1
  27.3 3.0 all-to-all-done.1
  30.3 2.8 all-to-all-start
  33.3 7.1 all-to-all-done
  43.2 5.3 multiply_reduce_fusion
  48.5 7.2 convolution_bitcast_fusion
  55.7 25.1 %copy.78 = f32[8,2,512,512]{3,1,0,2:T(2,128)} copy(f32[8,2,512,512]{2,3,1,0:T(8,128)} %convolution_bitcast_fusion) | data formatting | bytes 33554432 | tf_op jit(solution)/shard_map/while/body/eval_jaxpr/qrj,qrci->qcji/transpose | solution.py:94
  80.8 6.0 all-to-all-start.2
  87.2 3.9 fusion.60
  91.0 4.1 fusion.58
  97.8 173.0 %all-to-all-done.2 = f32[8,2,512,512]{3,1,0,2:T(2,128)} async-done(((f32[8,2,512,512]{3,1,0,2:T(2,128)}), f32[8,2,512,512]{3,1,0,2:T(2,128)}, u32[]{:S(2)}, u32[]{:S(2)}) %all-to-all-start.2) | async-done | bytes 16777248 | tf_op jit(solution)/shard_map/all_to_all | solution.py:110
  270.8 2.6 all-to-all-start.4
  273.4 11.0 %copy.79 = f32[8,2,512,512]{3,2,1,0:T(8,128)S(1)} copy(f32[8,2,512,512]{3,1,0,2:T(2,128)} %all-to-all-done.2) | data formatting | bytes 33554432 | tf_op jit(solution)/shard_map/all_to_all | solution.py:110
  284.4 6.7 copy.80
  291.1 42.0 %fusion.11 = f32[2,16,4,64,512]{4,1,3,2,0:T(8,128)} fusion(f32[16,4,2,64,512]{4,3,2,1,0:T(8,128)} %bitcast.109, f32[1,2,16,16]{3,2,1,0:T(8,128)S(1)} %get-tuple-element.44, f32[1,2,16,16]{3,2,1,0:T(8,128)S(1)} %get-tuple-element.43), kind=kOutput, calls=%fused_computation.23 | convolution fusion | flops 1610613760 | bytes 33558528 | tf_op jit(solution)/shard_map/acnt,tvcji->anvji/dot_general | solution.py:119
  333.1 7.1 multiply_subtract_fusion.1
  340.2 6.4 pad_maximum_fusion
  346.6 67.2 %fusion.14 = f32[2,512,16,4,64]{1,4,3,2,0:T(8,128)} fusion(f32[2,16,4,64,512]{4,1,3,2,0:T(8,128)} %pad_maximum_fusion, f32[1,2,512,512]{3,2,1,0:T(8,128)S(1)} %copy-done, f32[1,2,512,512]{3,2,1,0:T(8,128)S(1)} %get-tuple-element.34), kind=kOutput, calls=%fused_computation.24 | convolution fusion | flops 51540656128 | bytes 37748736 | tf_op jit(solution)/shard_map/acmi,cnvji->amnvj/dot_general | solution.py:128
  413.8 31.1 %copy.83 = f32[2,512,16,4,64]{4,3,2,1,0:T(4,128)} copy(f32[2,512,16,4,64]{1,4,3,2,0:T(8,128)} %fusion.14) | data formatting | bytes 33554432 | tf_op jit(solution)/shard_map/acmi,cnvji->amnvj/dot_general | solution.py:128
  444.9 27.4 %reshape.436 = f32[2,1,32,65536]{3,2,0,1:T(8,128)} reshape(f32[2,512,16,4,64]{4,3,2,1,0:T(4,128)} %copy.83) | data formatting | bytes 33554432 | tf_op jit(solution)/shard_map/reshape | solution.py:131
  472.2 28.6 %copy.84 = f32[2,1,32,65536]{3,0,1,2:T(2,128)} copy(f32[2,1,32,65536]{3,2,0,1:T(8,128)} %reshape.436) | data formatting | bytes 33554432 | tf_op jit(solution)/shard_map/reshape | solution.py:131
  500.9 6.0 all-to-all-start.3
  507.1 4.2 sine_negate_fusion
  516.5 363.0 %all-to-all-done.3 = f32[2,1,32,65536]{3,0,1,2:T(2,128)} async-done(((f32[2,1,32,65536]{3,0,1,2:T(2,128)}), f32[2,1,32,65536]{3,0,1,2:T(2,128)}, u32[]{:S(2)}, u32[]{:S(2)}) %all-to-all-start.3) | async-done | bytes 16777248 | tf_op jit(solution)/shard_map/all_to_all | solution.py:132
  879.5 38.4 %reshape.487 = f32[2,4,8,256,4,64]{5,4,3,0,2,1:T(4,128)} reshape(f32[2,1,32,65536]{3,0,1,2:T(2,128)} %all-to-all-done.3) | data formatting | bytes 33554432 | tf_op jit(solution)/shard_map/reshape | solution.py:133
  918.0 30.9 %copy.86 = f32[2,4,8,256,4,64]{3,4,1,0,5,2:T(4,128)} copy(f32[2,4,8,256,4,64]{5,4,3,0,2,1:T(4,128)} %reshape.487) | data formatting | bytes 33554432 | tf_op jit(solution)/shard_map/reshape | solution.py:133
  948.8 31.8 %fusion.17 = f32[2,16,8,256,64]{3,1,4,2,0:T(8,128)S(1)} fusion(f32[2,4,8,256,4,64]{3,4,1,0,5,2:T(4,128)} %copy.86, f32[2,2,16,4,4,1,1]{2,4,3,1,6,5,0:T(4,128)S(1)} %maximum_bitcast_fusion.17), kind=kOutput, calls=%fused_computation.25 | convolution fusion | flops 1610612736 | bytes 33558528 | tf_op jit(solution)/shard_map/acnpv,cptrvj->antrj/dot_general | solution.py:135
  980.6 2.8 multiply_subtract_fusion
  985.2 42.3 %fusion.10 = f32[256,512,16]{1,0,2:T(8,128)} fusion(f32[2,16,8,256,64]{3,1,4,2,0:T(8,128)S(1)} %pad_maximum_fusion.1, f32[1,512,8,64]{1,3,2,0:T(8,128)S(1)} %get-tuple-element.56, f32[1,512,8,64]{1,3,2,0:T(8,128)S(1)} %get-tuple-element.57), kind=kOutput, calls=%fused_computation.18 | convolution fusion | flops 25772425216 | bytes 27262976 | tf_op jit(solution)/shard_map/cmtj,cntrj->rmn/dot_general | solution.py:145
  1027.6 10.3 copy.88
  1037.9 8.9 copy.92
  (60 shorter events, 28.0 us)
Async XLA Ops:
  11.4 14.1 %copy-start.1 = (s32[512]{0:T(512)}, s32[512]{0:T(512)S(1)}, u32[]{:S(2)}) copy-start(s32[512]{0:T(512)S(1)} %compare_select_fusion) | copy-start | bytes 6148
  14.8 15.5 %all-to-all-start.1 = ((s32[2,8,32,4]{1,3,0,2:T(4,128)}), s32[2,8,32,4]{1,3,0,2:T(4,128)S(1)}, u32[]{:S(2)}, u32[]{:S(2)}) async-start(s32[2,8,32,4]{1,3,0,2:T(4,128)} %copy.70), calls=%async_computation.1 | async-start | bytes 262144 | tf_op jit(solution)/shard_map/all_to_all | solution.py:69
  30.3 10.1 all-to-all-start
  80.8 190.0 %all-to-all-start.2 = ((f32[8,2,512,512]{3,1,0,2:T(2,128)}), f32[8,2,512,512]{3,1,0,2:T(2,128)}, u32[]{:S(2)}, u32[]{:S(2)}) async-start(f32[8,2,512,512]{3,1,0,2:T(2,128)} %copy.78), calls=%async_computation.2 | async-start | bytes 33554432 | tf_op jit(solution)/shard_map/all_to_all | solution.py:110
  270.8 230.0 %all-to-all-start.4 = ((f32[2,8,32,4]{1,3,0,2:T(4,128)}), f32[2,8,32,4]{1,3,0,2:T(4,128)S(1)}, u32[]{:S(2)}, u32[]{:S(2)}) async-start(f32[2,8,32,4]{1,3,0,2:T(4,128)} %copy.90), calls=%async_computation.4 | async-start | bytes 262144 | tf_op jit(solution)/shard_map/all_to_all | solution.py:102
  340.2 6.4 copy-start
  500.9 6.0 copy-start.2
  500.9 378.7 %all-to-all-start.3 = ((f32[2,1,32,65536]{3,0,1,2:T(2,128)}), f32[2,1,32,65536]{3,0,1,2:T(2,128)}, u32[]{:S(2)}, u32[]{:S(2)}) async-start(f32[2,1,32,65536]{3,0,1,2:T(2,128)} %copy.84), calls=%async_computation.3 | async-start | bytes 33554432 | tf_op jit(solution)/shard_map/all_to_all | solution.py:132
where the time goes:
time: 1060 us; the launch traced here: 1050 us
  waiting for transfers between devices  546 us (52%)
  local copies, waits for them, and re-layouts  235 us (22%)
  matrix products  196 us (18%)
  other arithmetic  44 us (4%)
  starting transfers between devices  24.7 us (2%)
    all_to_all x1, waiting for transfers between devices, on_device(): lax.all_to_all(packed, ('blen', 'tm'), split_axis=2, concat_axis=1, tiled...  363 us
    all_to_all x1, waiting for transfers between devices, on_device(): lax.all_to_all(adjoint, 'tm', split_axis=2, concat_axis=0, tiled=True)  173 us
    reshape x2, local copies, waits for them, and re-layouts, on_device(): landed.reshape(2, blen_size, tm_size, rows_dev, tile_cols, col_slice)  69.3 us
    dot_general x1, matrix products, on_device(): jnp.einsum('acmi,cnvji->amnvj', tile_turn, turned, precision=highest)  67.2 us
    reshape x2, local copies, waits for them, and re-layouts, on_device(): packed = columns.reshape(2, 1, devices, spread_cols)  56 us
    dot_general x1, matrix products, on_device(): jnp.einsum('cmtj,cntrj->rmn', real_turn, turned_rows, precision=highest)  42.3 us
    dot_general x1, matrix products, on_device(): jnp.einsum('acnt,tvcji->anvji', small_turn, pieces, precision=highest)  42 us
    dot_general x1, matrix products, on_device(): jnp.einsum('acnpv,cptrvj->antrj', small_split, landed, precision=highest)  31.8 us
  transfers between devices with their start and end apart: 5, of which 4 were waited for; matrix products, arithmetic and copies ran while one was open for 24% of the time, Pallas kernels for 0%

commit v1 on v0

--- a/solution.py
+++ b/solution.py
@@ -10,6 +10,13 @@
 MOST = 4
 kernel_scale = 0.5
 highest = lax.Precision.HIGHEST
+
+
+def stacked_exchange(x, axis, split, join):
+    devices = lax.axis_size(axis)
+    pieces = jnp.stack(jnp.split(x, devices, axis=split), axis=0)
+    pieces = lax.all_to_all(pieces, axis, split_axis=0, concat_axis=0)
+    return jnp.concatenate(pieces, axis=join)
 
 
 def taps_full(offsets, fractions, tile_side):
@@ -129,7 +136,7 @@
     rows_dev = NPIX // devices
     spread_cols = rows_dev * tile_cols * col_slice
     packed = columns.reshape(2, 1, devices, spread_cols)
-    landed = lax.all_to_all(packed, ("blen", "tm"), split_axis=2, concat_axis=1, tiled=True)
+    landed = stacked_exchange(packed, ("blen", "tm"), 2, 1)
     landed = landed.reshape(2, blen_size, tm_size, rows_dev, tile_cols, col_slice)
     small_split = small_turn.reshape(2, 2, NT, blen_size, tile_cols)
     section_two = jnp.einsum("acnpv,cptrvj->antrj", small_split, landed, precision=highest)

time: 1060 us -> 1160 us (1.094)
  local copies, waits for them, and re-layouts: 235 us -> 345 us
    unnamed x11 -> x44, local copies, waits for them, and re-layouts: 12.5 us -> 87 us
    another operation x2 -> x5, local copies, waits for them, and re-layouts: 0.19 us -> 70.7 us  [the longest x2 69.3 us: on_device(): landed.reshape(2, blen_size, tm_size, rows_dev, tile_cols, col_slice)]
    reshape x2 -> x1, local copies, waits for them, and re-layouts: 56 us -> 27.4 us  [on_device(): packed = columns.reshape(2, 1, devices, spread_cols)]
    reshape x2 -> x1, local copies, waits for them, and re-layouts: 69.3 us -> 62.3 us  [stacked_exchange(): return jnp.concatenate(pieces, axis=join)]
  transfers between devices with their start and end apart: 5 -> 5, of which waited for: 4 -> 4; matrix products, arithmetic and copies ran while one was open for 24% -> 25% of each run, Pallas kernels for 0% -> 0%
where the time goes in v1:
time: 1160 us; the launch traced here: 1150 us
  waiting for transfers between devices  546 us (47%)
  local copies, waits for them, and re-layouts  345 us (30%)
  matrix products  187 us (16%)
  other arithmetic  44 us (4%)
  starting transfers between devices  24.6 us (2%)
    all_to_all x1, waiting for transfers between devices, stacked_exchange(): pieces = lax.all_to_all(pieces, axis, split_axis=0, concat_axis=0)  363 us
    all_to_all x1, waiting for transfers between devices, on_device(): lax.all_to_all(adjoint, 'tm', split_axis=2, concat_axis=0, tiled=True)  173 us
    unnamed x44, local copies, waits for them, and re-layouts  87 us
    another operation x2, local copies, waits for them, and re-layouts, on_device(): landed.reshape(2, blen_size, tm_size, rows_dev, tile_cols, col_slice)  69.3 us
    dot_general x1, matrix products, on_device(): jnp.einsum('acmi,cnvji->amnvj', tile_turn, turned, precision=highest)  67.2 us
    reshape x1, local copies, waits for them, and re-layouts, stacked_exchange(): return jnp.concatenate(pieces, axis=join)  62.3 us
    dot_general x1, matrix products, on_device(): jnp.einsum('cmtj,cntrj->rmn', real_turn, turned_rows, precision=highest)  42.3 us
    dot_general x1, matrix products, on_device(): jnp.einsum('acnt,tvcji->anvji', small_turn, pieces, precision=highest)  33.2 us
  transfers between devices with their start and end apart: 5, of which 4 were waited for; matrix products, arithmetic and copies ran while one was open for 25% of the time, Pallas kernels for 0%

profile of v1, /device:TPU:0, one launch (start us, length us, event | category | flops | bytes accessed | tf_op | source)
XLA Modules:
  0.0 1147.7 jit_solution(14902994199805064292)
XLA Ops:
  3.0 4.4 sort.17
  14.8 7.3 all-to-all-start.1
  33.3 7.1 all-to-all-done
  43.2 5.3 multiply_reduce_fusion
  48.5 7.2 convolution_bitcast_fusion
  55.7 25.1 %copy.140 = f32[8,2,512,512]{3,1,0,2:T(2,128)} copy(f32[8,2,512,512]{2,3,1,0:T(8,128)} %convolution_bitcast_fusion) | data formatting | bytes 33554432 | tf_op jit(solution)/shard_map/while/body/eval_jaxpr/qrj,qrci->qcji/transpose | solution.py:101
  80.8 5.9 all-to-all-start.2
  87.1 3.9 fusion.92
  90.9 4.1 fusion.90
  97.7 173.0 %all-to-all-done.2 = f32[8,2,512,512]{3,1,0,2:T(2,128)} async-done(((f32[8,2,512,512]{3,1,0,2:T(2,128)}), f32[8,2,512,512]{3,1,0,2:T(2,128)}, u32[]{:S(2)}, u32[]{:S(2)}) %all-to-all-start.2) | async-done | bytes 16777248 | tf_op jit(solution)/shard_map/all_to_all | solution.py:117
  273.3 11.0 copy.141
  284.3 6.7 copy.142
  291.0 33.2 %fusion.11 = f32[2,16,4,64,512]{4,1,3,2,0:T(8,128)} fusion(f32[16,4,2,64,512]{4,3,2,1,0:T(8,128)} %bitcast.301, f32[1,2,16,16]{3,2,1,0:T(8,128)S(1)} %get-tuple-element.44, f32[1,2,16,16]{3,2,1,0:T(8,128)S(1)} %get-tuple-element.43), kind=kOutput, calls=%fused_computation.24 | convolution fusion | flops 1610613760 | bytes 33558528 | tf_op jit(solution)/shard_map/acnt,tvcji->anvji/dot_general | solution.py:126
  324.2 7.1 multiply_subtract_fusion.1
  331.3 6.4 pad_maximum_fusion
  337.7 67.2 %fusion.14 = f32[2,512,16,4,64]{1,4,3,2,0:T(8,128)} fusion(f32[2,16,4,64,512]{4,1,3,2,0:T(8,128)} %pad_maximum_fusion, f32[1,2,512,512]{3,2,1,0:T(8,128)S(1)} %copy-done.1, f32[1,2,512,512]{3,2,1,0:T(8,128)S(1)} %get-tuple-element.34), kind=kOutput, calls=%fused_computation.25 | convolution fusion | flops 51540656128 | bytes 37748736 | tf_op jit(solution)/shard_map/acmi,cnvji->amnvj/dot_general | solution.py:135
  404.9 31.1 %copy.145 = f32[2,512,16,4,64]{4,3,2,1,0:T(4,128)} copy(f32[2,512,16,4,64]{1,4,3,2,0:T(8,128)} %fusion.14) | data formatting | bytes 33554432 | tf_op jit(solution)/shard_map/acmi,cnvji->amnvj/dot_general | solution.py:135
  436.0 27.4 %reshape.432 = f32[2,1,32,65536]{3,2,0,1:T(8,128)} reshape(f32[2,512,16,4,64]{4,3,2,1,0:T(4,128)} %copy.145) | data formatting | bytes 33554432 | tf_op jit(solution)/shard_map/reshape | solution.py:138
  466.8 4.2 fusion.88
  471.0 3.5 fusion.87
  474.5 3.5 fusion.86
  508.8 3.5 fusion.76
  539.1 6.0 all-to-all-start.3
  545.3 4.2 sine_negate_fusion
  554.7 363.0 %all-to-all-done.3 = f32[32,2,1,1,65536]{4,3,2,1,0:T(1,128)} async-done(((f32[32,2,1,1,65536]{4,3,2,1,0:T(1,128)}), f32[32,2,1,1,65536]{4,3,2,1,0:T(1,128)}, u32[]{:S(2)}, u32[]{:S(2)}) %all-to-all-start.3) | async-done | bytes 16777248 | tf_op jit(solution)/shard_map/all_to_all | solution.py:18
  917.8 62.3 %bitcast_reduce_fusion = f32[2,32,65536]{2,0,1:T(2,128)} fusion(f32[32,2,1,1,65536]{4,3,2,1,0:T(1,128)} %all-to-all-done.3), kind=kLoop, calls=%fused_computation.8 | loop fusion | bytes 33554432 | tf_op jit(solution)/shard_map/reshape | solution.py:19
  980.1 38.4 %reshape.483 = f32[2,4,8,256,4,64]{5,4,3,0,2,1:T(4,128)} reshape(f32[2,32,65536]{2,0,1:T(2,128)} %bitcast_reduce_fusion) | data formatting | bytes 33554432 | tf_op jit(solution)/shard_map/reshape;reshape | solution.py:140
  1018.5 30.9 %copy.178 = f32[2,4,8,256,4,64]{3,4,1,0,5,2:T(4,128)} copy(f32[2,4,8,256,4,64]{5,4,3,0,2,1:T(4,128)} %reshape.483) | data formatting | bytes 33554432 | tf_op jit(solution)/shard_map/reshape;reshape | solution.py:140
  1049.4 32.0 %fusion.17 = f32[2,16,8,256,64]{3,1,4,2,0:T(8,128)S(1)} fusion(f32[2,4,8,256,4,64]{3,4,1,0,5,2:T(4,128)} %copy.178, f32[2,2,16,4,4,1,1]{2,4,3,1,6,5,0:T(4,128)S(1)} %maximum_bitcast_fusion.17), kind=kOutput, calls=%fused_computation.26 | convolution fusion | flops 1610612736 | bytes 33558528 | tf_op jit(solution)/shard_map/acnpv,cptrvj->antrj/dot_general | solution.py:142
  1086.1 42.3 %fusion.10 = f32[256,512,16]{1,0,2:T(8,128)} fusion(f32[2,16,8,256,64]{3,1,4,2,0:T(8,128)S(1)} %pad_maximum_fusion.1, f32[1,512,8,64]{1,3,2,0:T(8,128)S(1)} %get-tuple-element.56, f32[1,512,8,64]{1,3,2,0:T(8,128)S(1)} %get-tuple-element.57), kind=kOutput, calls=%fused_computation.19 | convolution fusion | flops 25772425216 | bytes 27262976 | tf_op jit(solution)/shard_map/cmtj,cntrj->rmn/dot_general | solution.py:152
  1128.4 10.3 copy.180
  1138.6 8.9 copy.184
  (94 shorter events, 100.3 us)
Async XLA Ops:
  11.4 14.1 %copy-start.2 = (s32[512]{0:T(512)}, s32[512]{0:T(512)S(1)}, u32[]{:S(2)}) copy-start(s32[512]{0:T(512)S(1)} %compare_select_fusion) | copy-start | bytes 6148
  14.8 15.5 %all-to-all-start.1 = ((s32[2,8,32,4]{1,3,0,2:T(4,128)}), s32[2,8,32,4]{1,3,0,2:T(4,128)S(1)}, u32[]{:S(2)}, u32[]{:S(2)}) async-start(s32[2,8,32,4]{1,3,0,2:T(4,128)} %copy.132), calls=%async_computation.1 | async-start | bytes 262144 | tf_op jit(solution)/shard_map/all_to_all | solution.py:76
  30.3 10.1 all-to-all-start
  80.8 189.9 %all-to-all-start.2 = ((f32[8,2,512,512]{3,1,0,2:T(2,128)}), f32[8,2,512,512]{3,1,0,2:T(2,128)}, u32[]{:S(2)}, u32[]{:S(2)}) async-start(f32[8,2,512,512]{3,1,0,2:T(2,128)} %copy.140), calls=%async_computation.2 | async-start | bytes 33554432 | tf_op jit(solution)/shard_map/all_to_all | solution.py:117
  270.7 268.4 %all-to-all-start.4 = ((f32[2,8,32,4]{1,3,0,2:T(4,128)}), f32[2,8,32,4]{1,3,0,2:T(4,128)S(1)}, u32[]{:S(2)}, u32[]{:S(2)}) async-start(f32[2,8,32,4]{1,3,0,2:T(4,128)} %copy.182), calls=%async_computation.4 | async-start | bytes 262144 | tf_op jit(solution)/shard_map/all_to_all | solution.py:109
  331.3 6.4 copy-start.1
  463.4 55.7 %copy-start = (f32[2,1,32,65536]{3,2,0,1:T(8,128)S(1)}, f32[2,1,32,65536]{3,2,0,1:T(8,128)}, u32[]{:S(2)}) copy-start(f32[2,1,32,65536]{3,2,0,1:T(8,128)} %reshape.432) | copy-start | bytes 50331652
  539.1 6.0 copy-start.3
  539.1 378.7 %all-to-all-start.3 = ((f32[32,2,1,1,65536]{4,3,2,1,0:T(1,128)}), f32[32,2,1,1,65536]{4,3,2,1,0:T(1,128)}, u32[]{:S(2)}, u32[]{:S(2)}) async-start(f32[32,2,1,1,65536]{4,3,2,1,0:T(1,128)} %fusion.58), calls=%async_computation.3 | async-start | bytes 33554432 | tf_op jit(solution)/shard_map/all_to_all | solution.py:18
